TPU v7x, 32 devices: a whole 2x2x4 slice. The times are simulated.
32 devices in a mesh: dom: 4 (over z), lev: 4 (over y, x), mem: 2 (over core).
Axes of the slice: x: 2, y: 2, z: 4, core: 2. Of those that a mesh axis runs over, the one named last changes fastest.
Arguments:
- node_state: bfloat16 [2, 4, 32, 128, 128], P('mem', 'lev', 'dom'), may hold values from -6 to 6
- state_cotangent: bfloat16 [2, 4, 32, 128, 128], P('mem', 'lev', 'dom'), may hold values from -6 to 6
- edge_first: bfloat16 [256, 128], replicated, may hold values from -0.375 to 0.375
- edge_second: bfloat16 [128, 128], replicated, may hold values from -0.5 to 0.5
- node_first: bfloat16 [384, 128], replicated, may hold values from -0.3125 to 0.3125
- node_second: bfloat16 [128, 128], replicated, may hold values from -0.5 to 0.5
- inner_count: int32 [4], P('dom'), may hold values from 8 to 16, as said below
- inner_pairs: int32 [64, 2], P('dom'), may hold values from 0 to 7, as said below
- outer_pairs: int32 [32, 2], P('dom'), may hold values from 0 to 3
Outputs:
- updated: bfloat16 [2, 4, 32, 128, 128], P('mem', 'lev', 'dom')
- state_grad: bfloat16 [2, 4, 32, 128, 128], P('mem', 'lev', 'dom')
- edge_first_grad: float32 [256, 128], replicated
- edge_second_grad: float32 [128, 128], replicated
- node_first_grad: float32 [384, 128], replicated
- node_second_grad: float32 [128, 128], replicated
Inputs may be any that keep to these rules, and one draw needn't show every extreme that they name: `inner_count`: every entry lies between 8 and 16; some partition has exactly 16 live slots and some exactly 8; slots at and past the count hold valid block pairs that carry no flux. `inner_pairs`: the two block indices of a slot differ.
All inputs are finite; a program needn't handle non-finite values.
Results may differ from a plain program's by a relative error of at most 0.008.
Values may be sent and summed in bfloat16 or wider, within the bound.
A program may use at most 64 MiB of HBM per device.

v0:
```python
import math

import jax
import jax.numpy as jnp
from jax import lax
from jax.sharding import PartitionSpec as P

BND = 4
REACH = 2


precise_mode = lax.Precision.HIGHEST


def passed_along(value, axis, steps):
    count = lax.axis_size(axis)
    pairs = [(source, (source + steps) % count) for source in range(count)]
    return lax.ppermute(value, axis, pairs)


def swish_slope(pre_value):
    sigmoid_val = jax.nn.sigmoid(pre_value)
    return sigmoid_val * (1.0 + pre_value * (1.0 - sigmoid_val))


def widen_rows(piece, blocks):
    return jnp.pad(piece, ((0, 0), (0, blocks - piece.shape[1]), (0, 0), (0, 0)))


def edge_forward(left_rows, right_rows, edge_first, edge_second):
    inputs = jnp.concatenate(
        [
            jnp.concatenate([left_rows, right_rows], -1),
            jnp.concatenate([right_rows, left_rows], -1),
        ],
        axis=0,
    )
    pre_act = jnp.einsum("lfnk,kj->lfnj", inputs, edge_first, preferred_element_type=jnp.float32)
    hidden = jax.nn.silu(pre_act).astype(jnp.bfloat16)
    phi_out = jnp.einsum("lfnk,kj->lfnj", hidden, edge_second, preferred_element_type=jnp.float32)
    levels_here = left_rows.shape[0]
    return (phi_out[:levels_here] - phi_out[levels_here:], inputs, pre_act, hidden)


def edge_backward(face_grad, inputs, pre_act, hidden, edge_first, edge_second):
    levels_here = face_grad.shape[0]
    feat_width = edge_second.shape[0]
    signed = jnp.concatenate([face_grad, -face_grad], axis=0)
    act_slope = jnp.einsum("lfnj,kj->lfnk", signed, edge_second, preferred_element_type=jnp.float32)
    pre_grad = (act_slope * swish_slope(pre_act)).astype(jnp.bfloat16)
    grad_second = jnp.einsum("lfnk,lfnj->kj", hidden, signed, preferred_element_type=jnp.float32)
    grad_first = jnp.einsum("lfnk,lfnj->kj", inputs, pre_grad, preferred_element_type=jnp.float32)
    input_grad = jnp.einsum(
        "lfnj,kj->lfnk", pre_grad, edge_first, preferred_element_type=jnp.float32
    )
    left_grad = (
        input_grad[:levels_here, ..., :feat_width] + input_grad[levels_here:, ..., feat_width:]
    )
    right_grad = (
        input_grad[:levels_here, ..., feat_width:] + input_grad[levels_here:, ..., :feat_width]
    )
    return (left_grad, right_grad, grad_first, grad_second)


def shards(
    node_state,
    state_cotangent,
    edge_first,
    edge_second,
    node_first,
    node_second,
    inner_count,
    inner_pairs,
    outer_pairs,
):
    states = node_state[0]
    cotangent = state_cotangent[0]
    levels_here, blocks, row_count, feat_width = states.shape
    levels = levels_here * lax.axis_size("lev")
    inner_faces = inner_pairs.shape[0]
    outer_faces = outer_pairs.shape[0]
    per_offset = outer_faces // REACH
    active = (jnp.arange(inner_faces, dtype=jnp.int32) < inner_count[0]).astype(jnp.float32)
    face_weights = jnp.concatenate([active, jnp.ones((outer_faces,), jnp.float32)])
    left_index = jnp.concatenate([inner_pairs[:, 0], outer_pairs[:, 0]])
    right_index = jnp.concatenate([inner_pairs[:, 1], jnp.full((outer_faces,), blocks, jnp.int32)])
    left_table = jax.nn.one_hot(left_index, blocks, dtype=jnp.float32).T
    right_table = jax.nn.one_hot(right_index, blocks, dtype=jnp.float32).T
    signed_table = (left_table - right_table) * face_weights[None, :]
    remote_picks = [
        outer_pairs[(offset - 1) * per_offset : offset * per_offset, 1]
        for offset in range(1, REACH + 1)
    ]
    back_tables = [jax.nn.one_hot(picks, BND, dtype=jnp.float32).T for picks in remote_picks]
    edge_rows = states[:, :BND]
    remote_parts = []
    for offset in range(1, REACH + 1):
        halo_block = passed_along(edge_rows, "dom", -offset)
        remote_parts.append(jnp.take(halo_block, remote_picks[offset - 1], axis=1))
    left_rows = jnp.take(states, left_index, axis=1)
    right_rows = jnp.concatenate(
        [jnp.take(states, inner_pairs[:, 1], axis=1)] + remote_parts, axis=1
    )
    face_flux, inputs, pre_act, hidden = edge_forward(
        left_rows, right_rows, edge_first, edge_second
    )
    node_flux = jnp.einsum("bf,lfnh->lbnh", signed_table, face_flux, precision=precise_mode)
    for offset in range(1, REACH + 1):
        start = inner_faces + (offset - 1) * per_offset
        flux_part = face_flux[:, start : start + per_offset]
        outgoing = jnp.einsum(
            "bf,lfnh->lbnh", -back_tables[offset - 1], flux_part, precision=precise_mode
        )
        returned = passed_along(outgoing, "dom", offset)
        node_flux = node_flux + widen_rows(returned, blocks)
    local_depth = jnp.sum(node_flux, axis=0)
    depth_share = lax.psum_scatter(local_depth, "lev", scatter_dimension=0, tiled=True)
    depth_mean = lax.all_gather(
        (depth_share / levels).astype(jnp.bfloat16), "lev", axis=0, tiled=True
    )
    joined = jnp.concatenate([states, node_flux.astype(jnp.bfloat16), depth_mean[None]], -1)
    node_pre = jnp.einsum("lbnk,kj->lbnj", joined, node_first, preferred_element_type=jnp.float32)
    node_hidden = jax.nn.silu(node_pre).astype(jnp.bfloat16)
    updated = (
        states.astype(jnp.float32)
        + jnp.einsum("lbnk,kj->lbnj", node_hidden, node_second, preferred_element_type=jnp.float32)
    ).astype(jnp.bfloat16)
    act_slope = jnp.einsum(
        "lbnj,kj->lbnk", cotangent, node_second, preferred_element_type=jnp.float32
    )
    node_grad = (act_slope * swish_slope(node_pre)).astype(jnp.bfloat16)
    node_second_grad = jnp.einsum(
        "lbnk,lbnj->kj", node_hidden, cotangent, preferred_element_type=jnp.float32
    )
    node_first_grad = jnp.einsum(
        "lbnk,lbnj->kj", joined, node_grad, preferred_element_type=jnp.float32
    )
    joined_grad = jnp.einsum(
        "lbnj,kj->lbnk", node_grad, node_first, preferred_element_type=jnp.float32
    )
    state_grad = cotangent.astype(jnp.float32) + joined_grad[..., :feat_width]
    local_mean_grad = jnp.sum(joined_grad[..., 2 * feat_width :], axis=0)
    mean_share = lax.psum_scatter(local_mean_grad, "lev", scatter_dimension=0, tiled=True)
    mean_grad = lax.all_gather(
        (mean_share / levels).astype(jnp.bfloat16), "lev", axis=0, tiled=True
    )
    flux_grad_node = (
        joined_grad[..., feat_width : 2 * feat_width] + mean_grad.astype(jnp.float32)[None]
    )
    face_grad = jnp.einsum("bf,lbnh->lfnh", signed_table, flux_grad_node, precision=precise_mode)
    remote_grads = []
    for offset in range(1, REACH + 1):
        halo_grad = passed_along(
            flux_grad_node[:, :BND].astype(jnp.bfloat16), "dom", -offset
        ).astype(jnp.float32)
        remote_grads.append(jnp.take(halo_grad, remote_picks[offset - 1], axis=1))
    face_grad = face_grad - jnp.concatenate(
        [jnp.zeros((levels_here, inner_faces, row_count, feat_width), jnp.float32)] + remote_grads,
        axis=1,
    )
    face_grad = face_grad.astype(jnp.bfloat16)
    left_grad, right_grad, edge_first_grad, edge_second_grad = edge_backward(
        face_grad, inputs, pre_act, hidden, edge_first, edge_second
    )
    state_grad = state_grad + jnp.einsum(
        "bf,lfnh->lbnh", left_table, left_grad, precision=precise_mode
    )
    state_grad = state_grad + jnp.einsum(
        "bf,lfnh->lbnh", right_table, right_grad, precision=precise_mode
    )
    for offset in range(1, REACH + 1):
        start = inner_faces + (offset - 1) * per_offset
        outgoing = jnp.einsum(
            "bf,lfnh->lbnh",
            back_tables[offset - 1],
            right_grad[:, start : start + per_offset],
            precision=precise_mode,
        )
        returned = passed_along(outgoing.astype(jnp.bfloat16), "dom", offset).astype(outgoing.dtype)
        state_grad = state_grad + widen_rows(returned, blocks)
    edge_first_grad, edge_second_grad, node_first_grad, node_second_grad = lax.psum(
        (edge_first_grad, edge_second_grad, node_first_grad, node_second_grad),
        ("dom", "lev", "mem"),
    )
    grad_scale = 1.0 / math.sqrt(
        lax.axis_size("mem") * levels * blocks * lax.axis_size("dom") * row_count
    )
    return (
        updated[None],
        state_grad.astype(jnp.bfloat16)[None],
        edge_first_grad * grad_scale,
        edge_second_grad * grad_scale,
        node_first_grad * grad_scale,
        node_second_grad * grad_scale,
    )


def solution(mesh):
    placed = (
        P("mem", "lev", "dom", None, None),
        P("mem", "lev", "dom", None, None),
        P(),
        P(),
        P(),
        P(),
        P("dom"),
        P("dom", None),
        P("dom", None),
    )
    return jax.shard_map(
        shards,
        mesh=mesh,
        in_specs=placed,
        out_specs=(
            P("mem", "lev", "dom", None, None),
            P("mem", "lev", "dom", None, None),
            P(),
            P(),
            P(),
            P(),
        ),
        check_vma=False,
    )
```

profile of v0, /device:TPU:0, one launch (start us, length us, event | category | flops | bytes accessed | tf_op | source)
XLA Modules:
  0.0 294.1 jit_solution(14020146039758746296)
XLA Ops:
  7.2 1.2 copy.156
  8.5 4.1 %collective-permute-start.1 = (bf16[1,4,128,128]{3,1,2,0:T(4,128)(2,1)S(1)}, bf16[1,4,128,128]{3,1,2,0:T(4,128)(2,1)S(1)}, u32[]{:S(2)}, u32[]{:S(2)}) collective-permute-start(bf16[1,4,128,128]{3,1,2,0:T(4,128)(2,1)S(1)} %slice.95), channel_id=1, source_target_pairs={{0,16},{8,24},{16,0},{24,8},{1,17},{9,25},{17,1},{25,9},{2,18},{10... | collective-permute-start | bytes 393224 | tf_op jit(solution)/shard_map/ppermute | solution.py:18
  12.6 1.3 collective-permute-start
  13.9 0.8 compare_and_fusion.1
  14.8 0.7 slice_bitcast_fusion.8
  15.5 0.8 slice_bitcast_fusion.7
  16.2 0.7 and_bitcast_fusion
  16.9 0.8 slice_bitcast_fusion.6
  17.8 1.6 gather_fusion
  19.5 0.6 gather_fusion.1
  21.3 0.6 gather_fusion.3
  22.0 0.6 gather_fusion.2
  22.6 0.8 maximum_maximum_fusion
  23.5 2.7 multiply_convert_fusion.1
  26.2 0.5 fusion.60
  26.8 0.6 copy-done.4
  27.7 0.7 convolution_bitcast_fusion.2
  28.4 1.2 collective-permute-start.2
  29.7 0.7 convolution_bitcast_fusion.1
  30.4 3.4 %collective-permute-start.3 = (f32[1,4,128,128]{3,1,2,0:T(4,128)S(1)}, f32[1,4,128,128]{3,1,2,0:T(4,128)S(1)}, u32[]{:S(2)}, u32[]{:S(2)}) collective-permute-start(f32[1,4,128,128]{3,1,2,0:T(4,128)S(1)} %convolution_bitcast_fusion.1), channel_id=1, source_target_pairs={{0,16},{8,24},{16,0},{24,8},{1,17},{9,25},{17,1},{25,9},{2,18},{10... | collective-permute-start | bytes 786440 | tf_op jit(solution)/shard_map/ppermute | solution.py:18
  34.1 5.7 %collective-permute-done.2 = f32[1,4,128,128]{3,1,2,0:T(4,128)S(1)} collective-permute-done((f32[1,4,128,128]{3,1,2,0:T(4,128)S(1)}, f32[1,4,128,128]{3,1,2,0:T(4,128)S(1)}, u32[]{:S(2)}, u32[]{:S(2)}) %collective-permute-start.2) | collective-permute-done | bytes 262176 | tf_op jit(solution)/shard_map/ppermute | solution.py:18
  39.7 10.5 %collective-permute-done.3 = f32[1,4,128,128]{3,1,2,0:T(4,128)S(1)} collective-permute-done((f32[1,4,128,128]{3,1,2,0:T(4,128)S(1)}, f32[1,4,128,128]{3,1,2,0:T(4,128)S(1)}, u32[]{:S(2)}, u32[]{:S(2)}) %collective-permute-start.3) | collective-permute-done | bytes 262176 | tf_op jit(solution)/shard_map/ppermute | solution.py:18
  50.2 1.8 fusion.50
  52.0 0.9 copy.65
  53.0 23.4 %reduce-scatter.3.cloned.1.call-done = f32[2,128,128]{2,1,0:T(8,128)} async-done(((f32[8,128,128]{2,1,0:T(8,128)}), f32[2,128,128]{2,1,0:T(8,128)}) %reduce-scatter.3.cloned.1.call-update) | async-done | bytes 131088 | tf_op jit(solution)/shard_map/reduce_scatter | solution.py:117
  76.4 0.9 multiply_convert_fusion.4
  77.4 9.2 %all_gather.6 = bf16[8,128,128]{2,1,0:T(8,128)(2,1)S(1)} all-gather(bf16[2,128,128]{2,1,0:T(8,128)(2,1)S(1)} %multiply_convert_fusion.4), channel_id=1, replica_groups=mesh['dom'=4,'lev'=4,'mem'=2] {'lev'}, dimensions={0}, use_global_device_ids=true | all-gather | bytes 327680 | tf_op jit(solution)/shard_map/all_gather | solution.py:118
  87.3 0.4 copy-done.6
  88.1 0.7 copy-done.9
  89.1 0.9 slice_bitcast_fusion
  90.1 0.5 pad.30.clone
  90.6 1.7 fusion.20
  92.3 1.1 convolution_bitcast_fusion.3
  93.5 21.8 %reduce-scatter.5.cloned.1.call-done = f32[2,128,128]{2,1,0:T(8,128)} async-done(((f32[8,128,128]{2,1,0:T(8,128)}), f32[2,128,128]{2,1,0:T(8,128)}) %reduce-scatter.5.cloned.1.call-update) | async-done | bytes 131088 | tf_op jit(solution)/shard_map/reduce_scatter | solution.py:143
  115.2 0.9 multiply_convert_fusion.3
  116.2 9.2 %all_gather.7 = bf16[8,128,128]{2,1,0:T(8,128)(2,1)S(1)} all-gather(bf16[2,128,128]{2,1,0:T(8,128)(2,1)S(1)} %multiply_convert_fusion.3), channel_id=1, replica_groups=mesh['dom'=4,'lev'=4,'mem'=2] {'lev'}, dimensions={0}, use_global_device_ids=true | all-gather | bytes 327680 | tf_op jit(solution)/shard_map/all_gather | solution.py:144
  125.5 3.6 %collective-permute-start.4 = (bf16[1,4,128,128]{3,2,1,0:T(8,128)(2,1)S(1)}, bf16[1,4,128,128]{3,2,1,0:T(8,128)(2,1)S(1)}, u32[]{:S(2)}, u32[]{:S(2)}) collective-permute-start(bf16[1,4,128,128]{3,2,1,0:T(8,128)(2,1)S(1)} %slice.152), channel_id=1, source_target_pairs={{0,24},{8,0},{16,8},{24,16},{1,25},{9,1},{17,9},{25,17},{2,26},{10... | collective-permute-start | bytes 393224 | tf_op jit(solution)/shard_map/ppermute | solution.py:18
  129.0 1.0 convolution_bitcast_fusion.4
  130.1 1.5 collective-permute-done.4
  131.6 0.6 gather_fusion.4
  132.2 3.8 %collective-permute-done.5 = bf16[1,4,128,128]{3,2,1,0:T(8,128)(2,1)S(1)} collective-permute-done((bf16[1,4,128,128]{3,2,1,0:T(8,128)(2,1)S(1)}, bf16[1,4,128,128]{3,2,1,0:T(8,128)(2,1)S(1)}, u32[]{:S(2)}, u32[]{:S(2)}) %collective-permute-start.5) | collective-permute-done | bytes 131104 | tf_op jit(solution)/shard_map/ppermute | solution.py:18
  136.0 0.6 gather_fusion.5
  137.0 1.8 fusion.94
  138.9 1.2 copy-done.5
  140.2 1.2 fusion.26
  141.4 0.7 copy-done.28
  142.1 1.4 multiply_convert_fusion
  143.5 0.5 copy-done.3
  144.0 1.7 fusion.21
  145.7 1.0 fusion.55
  146.7 0.4 fusion.2
  147.4 0.5 fusion.45
  147.9 0.5 collective-permute-start.6
  148.4 0.5 fusion.43
  149.0 3.5 %collective-permute-start.7 = (bf16[1,4,128,128]{3,2,1,0:T(8,128)(2,1)S(1)}, bf16[1,4,128,128]{3,2,1,0:T(8,128)(2,1)S(1)}, u32[]{:S(2)}, u32[]{:S(2)}) collective-permute-start(bf16[1,4,128,128]{3,2,1,0:T(8,128)(2,1)S(1)} %bitcast.213), channel_id=1, source_target_pairs={{0,16},{8,24},{16,0},{24,8},{1,17},{9,25},{17,1},{25,9},{2,18},{10... | collective-permute-start | bytes 393224 | tf_op jit(solution)/shard_map/ppermute | solution.py:18
  152.4 1.5 fusion.10
  153.9 1.5 fusion.8
  155.5 4.0 %collective-permute-done.7 = bf16[1,4,128,128]{3,2,1,0:T(8,128)(2,1)S(1)} collective-permute-done((bf16[1,4,128,128]{3,2,1,0:T(8,128)(2,1)S(1)}, bf16[1,4,128,128]{3,2,1,0:T(8,128)(2,1)S(1)}, u32[]{:S(2)}, u32[]{:S(2)}) %collective-permute-start.7) | collective-permute-done | bytes 131104 | tf_op jit(solution)/shard_map/ppermute | solution.py:18
  159.5 0.9 fusion.39
  160.5 121.0 %all-reduce.9.cloned.1.call-done = (f32[256,128]{1,0:T(8,128)}, f32[128,128]{1,0:T(8,128)}, f32[384,128]{1,0:T(8,128)}, f32[128,128]{1,0:T(8,128)}) async-done(((f32[256,128]{1,0:T(8,128)}, f32[128,128]{1,0:T(8,128)}, f32[384,128]{1,0:T(8,128)}, f32[128,128]{1,0:T(8,128)}), (f32[256,128]{1,0:T(8,128)}, f32[128,128]{1,0:T(8,128)}, f32[384,128]{1,0:T(8,128)}, ...) | async-done | bytes 458768 | tf_op jit(solution)/shard_map/psum | solution.py:181
  281.5 1.6 broadcast_multiply_fusion
  283.1 1.6 broadcast_multiply_fusion.1
  284.7 1.5 broadcast_multiply_fusion.2
  286.1 1.5 broadcast_multiply_fusion.3
  (96 shorter events, 3.7 us)
Async XLA Ops:
  7.2 79.8 %copy-start = (bf16[384,128]{1,0:T(8,128)(2,1)S(1)}, bf16[384,128]{1,0:T(8,128)(2,1)}, u32[]{:S(2)}) copy-start(bf16[384,128]{1,0:T(8,128)(2,1)} %param.17) | copy-start | bytes 294916
  7.2 12.3 %copy-start.1 = (bf16[1,1,8,128,128]{4,3,2,1,0:T(8,128)(2,1)S(1)}, bf16[1,1,8,128,128]{4,3,2,1,0:T(8,128)(2,1)}, u32[]{:S(2)}) copy-start(bf16[1,1,8,128,128]{4,3,2,1,0:T(8,128)(2,1)} %param.13) | copy-start | bytes 786436
  7.2 69.2 %reduce-scatter.3.cloned.1.call-start = ((), (), s32[]{:S(2)}) async-start(), calls=%async_computation.2 | async-start | bytes 655360 | tf_op jit(solution)/shard_map/reduce_scatter | solution.py:117
  8.5 12.8 %collective-permute-start.1 = (bf16[1,4,128,128]{3,1,2,0:T(4,128)(2,1)S(1)}, bf16[1,4,128,128]{3,1,2,0:T(4,128)(2,1)S(1)}, u32[]{:S(2)}, u32[]{:S(2)}) collective-permute-start(bf16[1,4,128,128]{3,1,2,0:T(4,128)(2,1)S(1)} %slice.95), channel_id=1, source_target_pairs={{0,16},{8,24},{16,0},{24,8},{1,17},{9,25},{17,1},{25,9},{2,18},{10... | collective-permute-start | bytes 393224 | tf_op jit(solution)/shard_map/ppermute | solution.py:18
  12.6 8.7 %collective-permute-start = (bf16[1,4,128,128]{3,1,2,0:T(4,128)(2,1)S(1)}, bf16[1,4,128,128]{3,1,2,0:T(4,128)(2,1)S(1)}, u32[]{:S(2)}, u32[]{:S(2)}) collective-permute-start(bf16[1,4,128,128]{3,1,2,0:T(4,128)(2,1)S(1)} %slice.95), channel_id=1, source_target_pairs={{0,24},{8,0},{16,8},{24,16},{1,25},{9,1},{17,9},{25,17},{2,26},{10... | collective-permute-start | bytes 393224 | tf_op jit(solution)/shard_map/ppermute | solution.py:18
  17.7 9.9 %copy-start.16 = (s32[4]{0:T(128)}, s32[4]{0:T(128)S(1)}, u32[]{:S(2)}) copy-start(s32[4]{0:T(128)S(1)} %get-tuple-element.38) | copy-start | bytes 52
  17.7 11.9 %copy-start.14 = (s32[4]{0:T(128)}, s32[4]{0:T(128)S(1)}, u32[]{:S(2)}) copy-start(s32[4]{0:T(128)S(1)} %get-tuple-element.39) | copy-start | bytes 52
  20.9 29.3 %copy-start.18 = (s32[24]{0:T(128)}, s32[24]{0:T(128)S(1)}, u32[]{:S(2)}) copy-start(s32[24]{0:T(128)S(1)} %get-tuple-element.29) | copy-start | bytes 292
  21.2 29.0 %copy-start.24 = (f32[24]{0:T(128)}, f32[24]{0:T(128)S(1)}, u32[]{:S(2)}) copy-start(f32[24]{0:T(128)S(1)} %pad_convert_fusion) | copy-start | bytes 292
  21.2 29.0 %copy-start.21 = (s32[24]{0:T(128)}, s32[24]{0:T(128)S(1)}, u32[]{:S(2)}) copy-start(s32[24]{0:T(128)S(1)} %concatenate.67) | copy-start | bytes 292
  22.6 0.9 copy-start.11
  23.5 2.7 copy-start.2
  23.5 2.7 copy-start.13
  26.2 1.2 copy-start.4
  28.4 11.3 %collective-permute-start.2 = (f32[1,4,128,128]{3,1,2,0:T(4,128)S(1)}, f32[1,4,128,128]{3,1,2,0:T(4,128)S(1)}, u32[]{:S(2)}, u32[]{:S(2)}) collective-permute-start(f32[1,4,128,128]{3,1,2,0:T(4,128)S(1)} %convolution_bitcast_fusion.2), channel_id=1, source_target_pairs={{0,8},{8,16},{16,24},{24,0},{1,9},{9,17},{17,25},{25,1},{2,10},{10... | collective-permute-start | bytes 786440 | tf_op jit(solution)/shard_map/ppermute | solution.py:18
  30.4 19.8 %collective-permute-start.3 = (f32[1,4,128,128]{3,1,2,0:T(4,128)S(1)}, f32[1,4,128,128]{3,1,2,0:T(4,128)S(1)}, u32[]{:S(2)}, u32[]{:S(2)}) collective-permute-start(f32[1,4,128,128]{3,1,2,0:T(4,128)S(1)} %convolution_bitcast_fusion.1), channel_id=1, source_target_pairs={{0,16},{8,24},{16,0},{24,8},{1,17},{9,25},{17,1},{25,9},{2,18},{10... | collective-permute-start | bytes 786440 | tf_op jit(solution)/shard_map/ppermute | solution.py:18
  53.0 62.3 %reduce-scatter.5.cloned.1.call-start = ((), (), s32[]{:S(2)}) async-start(), calls=%async_computation.3 | async-start | bytes 655360 | tf_op jit(solution)/shard_map/reduce_scatter | solution.py:143
  86.8 1.0 copy-start.6
  86.8 0.9 copy-start.26
  88.0 0.7 copy-start.9
  90.0 2.3 copy-start.10
  90.0 191.4 %all-reduce.9.cloned.1.call-start = ((), (), s32[]{:S(2)}) async-start(), calls=%async_computation.4 | async-start | bytes 917504 | tf_op jit(solution)/shard_map/psum | solution.py:181
  93.4 35.6 %copy-start.7 = (bf16[1,1,8,128,128]{4,3,2,1,0:T(8,128)(2,1)S(1)}, bf16[1,1,8,128,128]{4,3,2,1,0:T(8,128)(2,1)}, u32[]{:S(2)}) copy-start(bf16[1,1,8,128,128]{4,3,2,1,0:T(8,128)(2,1)} %param.14) | copy-start | bytes 786436
  125.5 6.1 %collective-permute-start.4 = (bf16[1,4,128,128]{3,2,1,0:T(8,128)(2,1)S(1)}, bf16[1,4,128,128]{3,2,1,0:T(8,128)(2,1)S(1)}, u32[]{:S(2)}, u32[]{:S(2)}) collective-permute-start(bf16[1,4,128,128]{3,2,1,0:T(8,128)(2,1)S(1)} %slice.152), channel_id=1, source_target_pairs={{0,24},{8,0},{16,8},{24,16},{1,25},{9,1},{17,9},{25,17},{2,26},{10... | collective-permute-start | bytes 393224 | tf_op jit(solution)/shard_map/ppermute | solution.py:18
  130.0 6.9 %copy-start.19 = (s32[24]{0:T(128)S(1)}, s32[24]{0:T(128)}, u32[]{:S(2)}) copy-start(s32[24]{0:T(128)} %copy-done.18) | copy-start | bytes 292
  130.0 6.9 %copy-start.22 = (s32[24]{0:T(128)S(1)}, s32[24]{0:T(128)}, u32[]{:S(2)}) copy-start(s32[24]{0:T(128)} %copy-done.21) | copy-start | bytes 292
  130.0 6.9 %copy-start.25 = (f32[24]{0:T(128)S(1)}, f32[24]{0:T(128)}, u32[]{:S(2)}) copy-start(f32[24]{0:T(128)} %copy-done.24) | copy-start | bytes 292
  130.0 7.0 %copy-start.27 = (f32[24]{0:T(128)S(1)}, f32[24]{0:T(128)}, u32[]{:S(2)}) copy-start(f32[24]{0:T(128)} %pad.30.clone) | copy-start | bytes 292
  130.0 5.9 %collective-permute-start.5 = (bf16[1,4,128,128]{3,2,1,0:T(8,128)(2,1)S(1)}, bf16[1,4,128,128]{3,2,1,0:T(8,128)(2,1)S(1)}, u32[]{:S(2)}, u32[]{:S(2)}) collective-permute-start(bf16[1,4,128,128]{3,2,1,0:T(8,128)(2,1)S(1)} %slice.152), channel_id=1, source_target_pairs={{0,16},{8,24},{16,0},{24,8},{1,17},{9,25},{17,1},{25,9},{2,18},{10... | collective-permute-start | bytes 393224 | tf_op jit(solution)/shard_map/ppermute | solution.py:18
  138.8 1.4 copy-start.5
  140.2 1.9 copy-start.28
  142.1 1.9 copy-start.3
  144.0 1.7 copy-start.12
  146.7 0.7 copy-start.17
  147.1 1.3 copy-start.15
  147.1 5.3 %copy-start.20 = (s32[24]{0:T(128)S(1)}, s32[24]{0:T(128)}, u32[]{:S(2)}) copy-start(s32[24]{0:T(128)} %copy-done.18) | copy-start | bytes 292
  147.9 6.1 %copy-start.23 = (s32[24]{0:T(128)S(1)}, s32[24]{0:T(128)}, u32[]{:S(2)}) copy-start(s32[24]{0:T(128)} %copy-done.21) | copy-start | bytes 292
  147.9 7.6 %collective-permute-start.6 = (bf16[1,4,128,128]{3,2,1,0:T(8,128)(2,1)S(1)}, bf16[1,4,128,128]{3,2,1,0:T(8,128)(2,1)S(1)}, u32[]{:S(2)}, u32[]{:S(2)}) collective-permute-start(bf16[1,4,128,128]{3,2,1,0:T(8,128)(2,1)S(1)} %bitcast.212), channel_id=1, source_target_pairs={{0,8},{8,16},{16,24},{24,0},{1,9},{9,17},{17,25},{25,1},{2,10},{10... | collective-permute-start | bytes 393224 | tf_op jit(solution)/shard_map/ppermute | solution.py:18
  149.0 10.5 %collective-permute-start.7 = (bf16[1,4,128,128]{3,2,1,0:T(8,128)(2,1)S(1)}, bf16[1,4,128,128]{3,2,1,0:T(8,128)(2,1)S(1)}, u32[]{:S(2)}, u32[]{:S(2)}) collective-permute-start(bf16[1,4,128,128]{3,2,1,0:T(8,128)(2,1)S(1)} %bitcast.213), channel_id=1, source_target_pairs={{0,16},{8,24},{16,0},{24,8},{1,17},{9,25},{17,1},{25,9},{2,18},{10... | collective-permute-start | bytes 393224 | tf_op jit(solution)/shard_map/ppermute | solution.py:18
  153.9 5.6 %copy-start.8 = (bf16[1,1,8,128,128]{4,3,2,1,0:T(8,128)(2,1)S(1)}, bf16[1,1,8,128,128]{4,3,2,1,0:T(8,128)(2,1)}, u32[]{:S(2)}) copy-start(bf16[1,1,8,128,128]{4,3,2,1,0:T(8,128)(2,1)} %param.14) | copy-start | bytes 786436
Sparse Core Ops, SparseCore 0:
  53.1 23.2 reduce-scatter.2
  90.1 25.0 reduce-scatter.4
  155.6 125.8 all-reduce.8
where the time goes:
time: 295 us; the launch traced here: 294 us
  waiting for transfers between devices  192 us (65%)
  matrix products  22.4 us (8%)
  blocking collectives  18.5 us (6%)
  starting transfers between devices  17.9 us (6%)
  between operations  15 us (5%)
  local copies, waits for them, and re-layouts  14.4 us (5%)
  other arithmetic  14.2 us (5%)
    psum x1, waiting for transfers between devices, shards(): lax.psum((edge_first_grad, edge_second_grad, node_first_grad, node_second...  121 us
    ppermute x8, waiting for transfers between devices, passed_along(): return lax.ppermute(value, axis, pairs)  25.4 us
    reduce_scatter x1, waiting for transfers between devices, shards(): lax.psum_scatter(local_depth, 'lev', scatter_dimension=0, tiled=True)  23.4 us
    reduce_scatter x1, waiting for transfers between devices, shards(): lax.psum_scatter(local_mean_grad, 'lev', scatter_dimension=0, tiled=True)  21.8 us
    ppermute x8, starting transfers between devices, passed_along(): return lax.ppermute(value, axis, pairs)  17.8 us
    all_gather x1, blocking collectives, shards(): lax.all_gather((depth_share / levels).astype(jnp.bfloat16), 'lev', axis=0...  9.24 us
    all_gather x1, blocking collectives, shards(): lax.all_gather((mean_share / levels).astype(jnp.bfloat16), 'lev', axis=0,...  9.22 us
  transfers between devices with their start and end apart: 11, of which 8 were waited for; matrix products, arithmetic and copies ran while one was open for 6% of the time, Pallas kernels for 0%

commit v1 on v0

v1 whole, which is shorter than its diff:
```python
import functools
import math

import jax
import jax.numpy as jnp
from jax import lax
from jax.experimental import pallas as pl
from jax.experimental.pallas import tpu as pltpu
from jax.sharding import PartitionSpec as P

BND = 4
REACH = 2
CHUNKS = 2
FWD_TILE = 32
BWD_TILE = 16
MESH = pl.DeviceIdType.MESH
F32 = jnp.float32
BF16 = jnp.bfloat16


def mm(a, b):
    return jnp.dot(a, b, preferred_element_type=F32)


def mm_nt(a, b):
    return lax.dot_general(a, b, (((1,), (1,)), ((), ())), preferred_element_type=F32)


def mm_tn(a, b):
    return lax.dot_general(a, b, (((0,), (0,)), ((), ())), preferred_element_type=F32)


def gate(z):
    return 0.5 * jnp.tanh(0.5 * z) + 0.5


def layer_kernel(
    sizes,
    offs,
    scale,
    count_ref,
    inner_ref,
    outer_ref,
    near1_ref,
    near2_ref,
    state_ref,
    cot_ref,
    ef_ref,
    es_ref,
    nf_ref,
    ns_ref,
    upd_ref,
    sgrad_ref,
    efg_ref,
    esg_ref,
    nfg_ref,
    nsg_ref,
    wd_s,
    wa_s,
    wc_s,
    wo_s,
    halo,
    tab,
    slope,
    nd,
    fluxb,
    frecv,
    meanb,
    pre,
    cotg,
    mpart,
    mrecv,
    mgrad,
    fpart,
    gw,
    gwsend,
    gwhalo,
    acc_a,
    acc_b,
    wacc,
    wsend,
    wrecv_n,
    wrecv_e,
    wdom_n,
    wdom_e,
    wfin,
    halo_ss,
    halo_rs,
    rs1_ss,
    rs1_rs,
    ag1_ss,
    ag1_rs,
    rs2_ss,
    rs2_rs,
    ag2_ss,
    ag2_rs,
    back_ss,
    back_rs,
    wr_ss,
    wr_rs,
    wd_ss,
    wd_rs,
    wg_ss,
    wg_rs,
):
    n_dom, n_lev, n_mem = sizes
    n_grp = n_lev * n_mem
    blocks, rows, h = state_ref.shape
    inner = inner_ref.shape[0]
    per = outer_ref.shape[0] // REACH
    chunk = rows // CHUNKS
    share = blocks // n_lev
    dom = lax.axis_index("dom")
    lev = lax.axis_index("lev")
    mem = lax.axis_index("mem")
    grp = lev * n_mem + mem

    def dom_dev(o):
        return {"dom": lax.rem(dom + o, n_dom), "lev": lev, "mem": mem}

    def lev_dev(k):
        return {"dom": dom, "lev": lax.rem(lev + k, n_lev), "mem": mem}

    def grp_id(k):
        return lax.rem(grp + k, n_grp)

    def grp_dev(k):
        g = grp_id(k)
        return {"dom": dom, "lev": g // n_mem, "mem": lax.rem(g, n_mem)}

    def remote(src, dst, ss, rs, dev):
        copy = pltpu.make_async_remote_copy(
            src_ref=src, dst_ref=dst, send_sem=ss, recv_sem=rs, device_id=dev, device_id_type=MESH
        )
        copy.start()
        return copy

    barrier = pltpu.get_barrier_semaphore()
    for o in range(1, n_dom):
        pl.semaphore_signal(barrier, inc=1, device_id=dom_dev(o), device_id_type=MESH)
    for k in range(1, n_grp):
        pl.semaphore_signal(barrier, inc=1, device_id=grp_dev(k), device_id_type=MESH)

    live = count_ref[0]
    for f in range(inner):
        m = jnp.where(f < live, 1.0, 0.0).astype(F32)
        a, c = inner_ref[f, 0], inner_ref[f, 1]
        for b in range(blocks):
            wa = jnp.where(a == b, m, 0.0)
            wc = jnp.where(c == b, m, 0.0)
            wa_s[f * blocks + b] = wa
            wc_s[f * blocks + b] = wc
            wd_s[f * blocks + b] = wa - wc
    outer = []
    for o in range(1, REACH + 1):
        near = near1_ref if o == 1 else near2_ref
        ahead = blocks + BND * offs.index(o % n_dom)
        behind = blocks + BND * offs.index(-o % n_dom)
        for j in range(per):
            outer.append((outer_ref[(o - 1) * per + j, 0], ahead + outer_ref[(o - 1) * per + j, 1]))
            outer.append((near[j, 1], behind + near[j, 0]))
    for f, (a, _) in enumerate(outer):
        for b in range(BND):
            wo_s[f * BND + b] = jnp.where(a == b, 1.0, 0.0).astype(F32)

    pl.semaphore_wait(barrier, n_dom - 1 + n_grp - 1)

    halo_c = []
    for c in range(CHUNKS):
        rc = pl.ds(c * chunk, chunk)
        halo_c.append(
            [
                remote(
                    state_ref.at[pl.ds(0, BND), rc],
                    halo.at[c, s],
                    halo_ss.at[c * len(offs) + s],
                    halo_rs.at[c * len(offs) + s],
                    dom_dev(n_dom - o),
                )
                for s, o in enumerate(offs)
            ]
        )

    ef_wide = jnp.concatenate([ef_ref[:h], ef_ref[h:]], axis=1)
    es = es_ref[...]
    ns = ns_ref[...]
    n0, n1, n2 = nf_ref[:h], nf_ref[h : 2 * h], nf_ref[2 * h :]

    def pair(f, ia, ic, at, size):
        ta = tab[ia, pl.ds(at, size), :]
        tc = tab[ic, pl.ds(at, size), :]
        z1 = ta[:, :h] + tc[:, h:]
        z2 = tc[:, :h] + ta[:, h:]
        g1, g2 = gate(z1), gate(z2)
        s1, s2 = z1 * g1, z2 * g2
        slope[f, 0, pl.ds(at, size), :] = g1 + s1 - s1 * g1
        slope[f, 1, pl.ds(at, size), :] = g2 + s2 - s2 * g2
        return s1 - s2

    def sum_faces(start, faces, table, width, base, at, size, load):
        acc = [nd[b, pl.ds(at, size), :] if load else None for b in range(width)]
        for f, (ia, ic) in enumerate(faces):
            d = pair(start + f, ia, ic, at, size)
            for b in range(width):
                term = table[f * width + b] * d
                acc[b] = term if acc[b] is None else acc[b] + term
        for b in range(width):
            nd[b, pl.ds(at, size), :] = acc[b]

    def tiles(c, size, body):
        def step(t, carry):
            body(pl.multiple_of(c * chunk + t * size, size))
            return carry

        lax.fori_loop(0, chunk // size, step, 0)

    def rows_of(ref, c):
        return ref[:, c * chunk : (c + 1) * chunk].reshape(-1, h)

    def put_rows(ref, c, value):
        ref[:, c * chunk : (c + 1) * chunk] = value.reshape(-1, chunk, value.shape[-1])

    inner_faces = [(inner_ref[f, 0], inner_ref[f, 1]) for f in range(inner)]
    for c in range(CHUNKS):
        tab[:blocks, c * chunk : (c + 1) * chunk] = mm(rows_of(state_ref, c), ef_wide).reshape(
            blocks, chunk, 2 * h
        )
        put_rows(cotg, c, mm_nt(rows_of(cot_ref, c), ns))
        put_rows(pre, c, mm(rows_of(state_ref, c), n0))
        tiles(
            c,
            FWD_TILE,
            lambda at: sum_faces(0, inner_faces, wd_s, blocks, 0, at, FWD_TILE, False),
        )

    def scatter(src, dst, ss, rs, c):
        out = []
        for k in range(1, n_lev):
            to = lax.rem(lev + k, n_lev)
            out.append(
                remote(
                    src.at[c, pl.ds(to * share, share)],
                    dst.at[c, k - 1],
                    ss.at[c * (n_lev - 1) + k - 1],
                    rs.at[c * (n_lev - 1) + k - 1],
                    lev_dev(k),
                )
            )
        return out

    def reduce_spread(copies, src, got, dst, ss, rs, c):
        for copy in copies:
            copy.wait_recv()
        mine = pl.ds(lev * share, share)
        total = src[c, mine].astype(F32)
        for k in range(n_lev - 1):
            total = total + got[c, k].astype(F32)
        dst[c, mine] = (total * (1.0 / n_lev)).astype(BF16)
        return [
            remote(
                dst.at[c, mine],
                dst.at[c, mine],
                ss.at[c * (n_lev - 1) + k - 1],
                rs.at[c * (n_lev - 1) + k - 1],
                lev_dev(k),
            )
            for k in range(1, n_lev)
        ]

    rs1 = []
    for c in range(CHUNKS):
        for copy in halo_c[c]:
            copy.wait_recv()
        tab[blocks:, c * chunk : (c + 1) * chunk] = mm(
            halo[c].reshape(-1, h), ef_wide
        ).reshape(-1, chunk, 2 * h)
        tiles(
            c,
            FWD_TILE,
            lambda at: sum_faces(inner, outer, wo_s, BND, 0, at, FWD_TILE, True),
        )
        fluxb[c] = mm(rows_of(nd, c).astype(BF16), es).astype(BF16).reshape(blocks, chunk, h)
        rs1.append(scatter(fluxb, frecv, rs1_ss, rs1_rs, c))
    ag1 = []
    for c in range(CHUNKS):
        put_rows(pre, c, rows_of(pre, c) + mm(fluxb[c].reshape(-1, h), n1))
        ag1.append(reduce_spread(rs1[c], fluxb, frecv, meanb, ag1_ss, ag1_rs, c))
    rs2 = []
    for c in range(CHUNKS):
        for copy in ag1[c]:
            copy.wait_recv()
        mean = meanb[c].reshape(-1, h)
        z = rows_of(pre, c) + mm(mean, n2)
        g = gate(z)
        s = z * g
        hidden = s.astype(BF16)
        grad = (rows_of(cotg, c) * (g + s - s * g)).astype(BF16)
        mpart[c] = mm_nt(grad, n2).astype(BF16).reshape(blocks, chunk, h)
        rs2.append(scatter(mpart, mrecv, rs2_ss, rs2_rs, c))
        state = rows_of(state_ref, c)
        cot = rows_of(cot_ref, c)
        put_rows(upd_ref, c, (state.astype(F32) + mm(hidden, ns)).astype(BF16))
        put_rows(pre, c, cot.astype(F32) + mm_nt(grad, n0))
        put_rows(fpart, c, mm_nt(grad, n1))
        parts = (
            mm_tn(state, grad),
            mm_tn(fluxb[c].reshape(-1, h), grad),
            mm_tn(mean, grad),
            mm_tn(hidden, cot),
        )
        for i, part in enumerate(parts):
            at = slice(i * h, (i + 1) * h)
            wacc[at] = part if c == 0 else wacc[at] + part
    ag2 = [
        reduce_spread(rs2[c], mpart, mrecv, mgrad, ag2_ss, ag2_rs, c) for c in range(CHUNKS)
    ]
    back = []
    for c in range(CHUNKS):
        for copy in ag2[c]:
            copy.wait_recv()
        grad = (rows_of(fpart, c) + mgrad[c].reshape(-1, h).astype(F32)).astype(BF16)
        wide = mm_nt(grad, es).reshape(blocks, chunk, h)
        gw[:blocks, c * chunk : (c + 1) * chunk] = wide
        gwsend[c] = wide[:BND].astype(BF16)
        back.append(
            [
                remote(
                    gwsend.at[c],
                    gwhalo.at[c, s],
                    back_ss.at[c * len(offs) + s],
                    back_rs.at[c * len(offs) + s],
                    dom_dev(n_dom - o),
                )
                for s, o in enumerate(offs)
            ]
        )
        part = mm_tn(rows_of(nd, c).astype(BF16), grad)
        at = slice(4 * h, 5 * h)
        wacc[at] = part if c == 0 else wacc[at] + part

    def weights_out(first, count, got, sem):
        size = count // n_grp
        wsend[first : first + count] = wacc[first : first + count].astype(BF16)
        return [
            remote(
                wsend.at[pl.ds(pl.multiple_of(first + grp_id(k) * size, 16), size)],
                got.at[k - 1],
                wr_ss.at[sem, k - 1],
                wr_rs.at[sem, k - 1],
                grp_dev(k),
            )
            for k in range(1, n_grp)
        ]

    def weights_mid(copies, first, count, got, held, sem):
        size = count // n_grp
        for copy in copies:
            copy.wait_recv()
        total = wacc[pl.ds(pl.multiple_of(first + grp * size, 16), size)]
        for k in range(n_grp - 1):
            total = total + got[k].astype(F32)
        held[dom] = total.astype(BF16)
        return [
            remote(
                held.at[dom],
                held.at[dom],
                wd_ss.at[sem, o - 1],
                wd_rs.at[sem, o - 1],
                dom_dev(o),
            )
            for o in range(1, n_dom)
        ]

    def weights_in(copies, first, count, held, sem):
        size = count // n_grp
        for copy in copies:
            copy.wait_recv()
        total = held[0].astype(F32)
        for o in range(1, n_dom):
            total = total + held[o].astype(F32)
        mine = pl.ds(pl.multiple_of(first + grp * size, 16), size)
        wfin[mine] = total.astype(BF16)
        return [
            remote(
                wfin.at[mine],
                wfin.at[mine],
                wg_ss.at[sem, k - 1],
                wg_rs.at[sem, k - 1],
                grp_dev(k),
            )
            for k in range(1, n_grp)
        ]

    def spread_faces(start, faces, width, at, size, load):
        aa = [acc_a[b, pl.ds(at, size), :] if load else None for b in range(width)]
        bb = [acc_b[b, pl.ds(at, size), :] if load else None for b in range(width)]

        def put(total, term):
            return term if total is None else total + term

        for f, (ia, ic) in enumerate(faces):
            t = gw[ia, pl.ds(at, size), :] - gw[ic, pl.ds(at, size), :]
            p1 = t * slope[start + f, 0, pl.ds(at, size), :]
            p2 = t * slope[start + f, 1, pl.ds(at, size), :]
            for b in range(width):
                if load:
                    w = wo_s[f * width + b]
                    aa[b] = put(aa[b], w * p1)
                    bb[b] = put(bb[b], -w * p2)
                else:
                    wa, wc = wa_s[f * width + b], wc_s[f * width + b]
                    aa[b] = put(aa[b], wa * p1 - wc * p2)
                    bb[b] = put(bb[b], wc * p1 - wa * p2)
        for b in range(width):
            acc_a[b, pl.ds(at, size), :] = aa[b]
            acc_b[b, pl.ds(at, size), :] = bb[b]

    n_rows = 5 * h
    w1 = weights_out(0, n_rows, wrecv_n, 0)
    for c in range(CHUNKS):
        tiles(c, BWD_TILE, lambda at: spread_faces(0, inner_faces, blocks, at, BWD_TILE, False))
        if c == 0:
            w2 = weights_mid(w1, 0, n_rows, wrecv_n, wdom_n, 0)
    for c in range(CHUNKS):
        for copy in back[c]:
            copy.wait_recv()
        gw[blocks:, c * chunk : (c + 1) * chunk] = (
            gwhalo[c].reshape(-1, chunk, h).astype(F32)
        )
        tiles(c, BWD_TILE, lambda at: spread_faces(inner, outer, BND, at, BWD_TILE, True))
        a = rows_of(acc_a, c).astype(BF16)
        b = rows_of(acc_b, c).astype(BF16)
        state = rows_of(state_ref, c)
        for i, part in enumerate((mm_tn(state, a), mm_tn(state, b))):
            at = slice((5 + i) * h, (6 + i) * h)
            wacc[at] = part if c == 0 else wacc[at] + part
        if c == CHUNKS - 1:
            e1 = weights_out(n_rows, 2 * h, wrecv_e, 1)
            w3 = weights_in(w2, 0, n_rows, wdom_n, 0)
        total = rows_of(pre, c) + mm_nt(a, ef_ref[:h]) + mm_nt(b, ef_ref[h:])
        put_rows(sgrad_ref, c, total.astype(BF16))
    e2 = weights_mid(e1, n_rows, 2 * h, wrecv_e, wdom_e, 1)
    for copy in w3:
        copy.wait_recv()
    nfg_ref[...] = wfin[: 3 * h].astype(F32) * scale
    nsg_ref[...] = wfin[3 * h : 4 * h].astype(F32) * scale
    esg_ref[...] = wfin[4 * h : 5 * h].astype(F32) * scale
    e3 = weights_in(e2, n_rows, 2 * h, wdom_e, 1)
    for group in halo_c + rs1 + ag1 + rs2 + ag2 + back + [w1, w2, w3, e1, e2]:
        for copy in group:
            copy.wait_send()
    for copy in e3:
        copy.wait()
    efg_ref[...] = wfin[5 * h :].astype(F32) * scale


def shards(
    node_state,
    state_cotangent,
    edge_first,
    edge_second,
    node_first,
    node_second,
    inner_count,
    inner_pairs,
    outer_pairs,
):
    state = node_state[0, 0]
    cot = state_cotangent[0, 0]
    blocks, rows, h = state.shape
    n_dom, n_lev, n_mem = (lax.axis_size(x) for x in ("dom", "lev", "mem"))
    n_grp = n_lev * n_mem
    inner = inner_pairs.shape[0]
    outer = outer_pairs.shape[0]
    per = outer // REACH
    offs = sorted({s * o % n_dom for o in range(1, REACH + 1) for s in (1, -1)})
    near = []
    for o in range(1, REACH + 1):
        hops = [(i, (i + o) % n_dom) for i in range(n_dom)]
        near.append(lax.ppermute(outer_pairs[(o - 1) * per : o * per], "dom", hops))
    scale = 1.0 / math.sqrt(n_mem * n_lev * blocks * n_dom * rows)
    faces = inner + 2 * outer
    chunk = rows // CHUNKS
    share = blocks // n_lev
    slots = len(offs)
    table = blocks + BND * slots
    size_n = 5 * h // n_grp
    size_e = 2 * h // n_grp
    dma = pltpu.SemaphoreType.DMA
    lev_sems = [dma((CHUNKS * (n_lev - 1),))] * 8
    full = (blocks, rows, h)
    cut = (CHUNKS, blocks, chunk, h)
    smem = pl.BlockSpec(memory_space=pltpu.SMEM)
    vmem = pl.BlockSpec(memory_space=pltpu.VMEM)
    upd, sgrad, efg, esg, nfg, nsg = pl.pallas_call(
        functools.partial(layer_kernel, (n_dom, n_lev, n_mem), offs, scale),
        out_shape=(
            jax.ShapeDtypeStruct(full, BF16),
            jax.ShapeDtypeStruct(full, BF16),
            jax.ShapeDtypeStruct((2 * h, h), F32),
            jax.ShapeDtypeStruct((h, h), F32),
            jax.ShapeDtypeStruct((3 * h, h), F32),
            jax.ShapeDtypeStruct((h, h), F32),
        ),
        in_specs=[smem] * 5 + [vmem] * 6,
        out_specs=(vmem,) * 6,
        scratch_shapes=[
            pltpu.SMEM((inner * blocks,), F32),
            pltpu.SMEM((inner * blocks,), F32),
            pltpu.SMEM((inner * blocks,), F32),
            pltpu.SMEM((2 * outer * BND,), F32),
            pltpu.VMEM((CHUNKS, slots, BND, chunk, h), BF16),
            pltpu.VMEM((table, rows, 2 * h), F32),
            pltpu.VMEM((faces, 2, rows, h), F32),
            pltpu.VMEM(full, F32),
            pltpu.VMEM(cut, BF16),
            pltpu.VMEM((CHUNKS, n_lev - 1, share, chunk, h), BF16),
            pltpu.VMEM(cut, BF16),
            pltpu.VMEM(full, F32),
            pltpu.VMEM(full, F32),
            pltpu.VMEM(cut, BF16),
            pltpu.VMEM((CHUNKS, n_lev - 1, share, chunk, h), BF16),
            pltpu.VMEM(cut, BF16),
            pltpu.VMEM(full, F32),
            pltpu.VMEM((table, rows, h), F32),
            pltpu.VMEM((CHUNKS, BND, chunk, h), BF16),
            pltpu.VMEM((CHUNKS, slots, BND, chunk, h), BF16),
            pltpu.VMEM(full, F32),
            pltpu.VMEM(full, F32),
            pltpu.VMEM((7 * h, h), F32),
            pltpu.VMEM((7 * h, h), BF16),
            pltpu.VMEM((n_grp - 1, size_n, h), BF16),
            pltpu.VMEM((n_grp - 1, size_e, h), BF16),
            pltpu.VMEM((n_dom, size_n, h), BF16),
            pltpu.VMEM((n_dom, size_e, h), BF16),
            pltpu.VMEM((7 * h, h), BF16),
            dma((CHUNKS * slots,)),
            dma((CHUNKS * slots,)),
            *lev_sems,
            dma((CHUNKS * slots,)),
            dma((CHUNKS * slots,)),
            dma((2, n_grp - 1)),
            dma((2, n_grp - 1)),
            dma((2, n_dom - 1)),
            dma((2, n_dom - 1)),
            dma((2, n_grp - 1)),
            dma((2, n_grp - 1)),
        ],
        compiler_params=pltpu.CompilerParams(
            collective_id=0, has_side_effects=True, vmem_limit_bytes=56 * 1024 * 1024
        ),
    )(
        inner_count,
        inner_pairs,
        outer_pairs,
        *near,
        state,
        cot,
        edge_first,
        edge_second,
        node_first,
        node_second,
    )
    return (upd[None, None], sgrad[None, None], efg, esg, nfg, nsg)


def solution(mesh):
    data = P("mem", "lev", "dom", None, None)
    return jax.shard_map(
        shards,
        mesh=mesh,
        in_specs=(data, data, P(), P(), P(), P(), P("dom"), P("dom", None), P("dom", None)),
        out_specs=(data, data, P(), P(), P(), P()),
        check_vma=False,
    )
```

time: 295 us -> 70.5 us (0.24)
  waiting for transfers between devices: 192 us -> 2.46 us
  Pallas kernels: 0 us -> 52.5 us
  matrix products: 22.4 us -> 0 us
  blocking collectives: 18.5 us -> 0 us
  other arithmetic: 14.2 us -> 0 us
  between operations: 15 us -> 1.32 us
  starting transfers between devices: 17.9 us -> 5.64 us
  local copies, waits for them, and re-layouts: 14.4 us -> 8.31 us
    psum x1 -> x0, waiting for transfers between devices: 121 us -> none  [shards(): lax.psum((edge_first_grad, edge_second_grad, node_first_grad, node_second...]
    pallas_call x0 -> x1, Pallas kernels: none -> 52.5 us  [shards(): pl.pallas_call(functools.partial(layer_kernel, (n_dom, n_lev, n_mem), off...]
    reduce_scatter x2 -> x0, waiting for transfers between devices: 45.2 us -> none  [the longest x1 23.4 us: shards(): lax.psum_scatter(local_depth, 'lev', scatter_dimension=0, tiled=True)]
    ppermute x8 -> x2, waiting for transfers between devices: 25.4 us -> 2.46 us  [shards(): near.append(lax.ppermute(outer_pairs[(o - 1) * per:o * per], 'dom', hops))]
    dot_general x20 -> x0, matrix products: 22.4 us -> none  [the longest x1 2.66 us: edge_forward(): jnp.einsum('lfnk,kj->lfnj', inputs, edge_first, preferred_element_type=jn...]
    all_gather x2 -> x0, blocking collectives: 18.5 us -> none  [the longest x1 9.24 us: shards(): lax.all_gather((depth_share / levels).astype(jnp.bfloat16), 'lev', axis=0...]
    ppermute x8 -> x2, starting transfers between devices: 17.8 us -> 5.64 us  [shards(): near.append(lax.ppermute(outer_pairs[(o - 1) * per:o * per], 'dom', hops))]
    mul x4 -> x0, other arithmetic: 6.14 us -> none  [the longest x1 1.62 us: shards(): node_first_grad * grad_scale]
  transfers between devices with their start and end apart: 11 -> 2, of which waited for: 8 -> 1; matrix products, arithmetic and copies ran while one was open for 6% -> 1% of each run, Pallas kernels for 0% -> 0%
where the time goes in v1:
time: 70.5 us; the launch traced here: 70.3 us
  Pallas kernels  52.5 us (74%)
  local copies, waits for them, and re-layouts  8.31 us (12%)
  starting transfers between devices  5.64 us (8%)
  waiting for transfers between devices  2.46 us (3%)
  between operations  1.32 us (2%)
    pallas_call x1, Pallas kernels, shards(): pl.pallas_call(functools.partial(layer_kernel, (n_dom, n_lev, n_mem), off...  52.5 us
    unnamed x26, local copies, waits for them, and re-layouts  8.3 us
    ppermute x2, starting transfers between devices, shards(): near.append(lax.ppermute(outer_pairs[(o - 1) * per:o * per], 'dom', hops))  5.64 us
    ppermute x2, waiting for transfers between devices, shards(): near.append(lax.ppermute(outer_pairs[(o - 1) * per:o * per], 'dom', hops))  2.46 us
  transfers between devices with their start and end apart: 2, of which 1 were waited for; matrix products, arithmetic and copies ran while one was open for 1% of the time, Pallas kernels for 0%

profile of v1, /device:TPU:0, one launch (start us, length us, event | category | flops | bytes accessed | tf_op | source)
XLA Modules:
  0.0 70.3 jit_solution(17482559002670654862)
XLA Ops:
  0.6 0.8 %copy.18.outer_ref = s32[8,2]{1,0:T(8,128)S(1)} copy(s32[8,2]{0,1:T(2,128)} %param.17) | data formatting | bytes 128 | tf_op args[8]
  1.4 0.0 copy-start.5
  1.4 0.6 copy-done.5
  2.0 4.1 %collective-permute-start.1 = (s32[4,2]{1,0:T(4,128)S(1)}, s32[4,2]{1,0:T(4,128)S(1)}, u32[]{:S(2)}, u32[]{:S(2)}) collective-permute-start(s32[4,2]{1,0:T(4,128)S(1)} %get-tuple-element.18), channel_id=1, source_target_pairs={{0,16},{8,24},{16,0},{24,8},{1,17},{9,25},{17,1},{25,9},{2,18},{10... | collective-permute-start | bytes 104 | tf_op jit(solution)/shard_map/ppermute | solution.py:480
  6.0 0.0 copy-start.8
  6.0 1.6 %collective-permute-start = (s32[4,2]{1,0:T(4,128)S(1)}, s32[4,2]{1,0:T(4,128)S(1)}, u32[]{:S(2)}, u32[]{:S(2)}) collective-permute-start(s32[4,2]{1,0:T(4,128)S(1)} %get-tuple-element.19), channel_id=1, source_target_pairs={{0,8},{8,16},{16,24},{24,0},{1,9},{9,17},{17,25},{25,1},{2,10},{10... | collective-permute-start | bytes 104 | tf_op jit(solution)/shard_map/ppermute | solution.py:480
  8.3 0.0 copy-done.8
  8.3 0.7 copy.17.inner_ref
  9.0 0.0 collective-permute-done.1.near2_ref
  9.0 0.0 copy-start.6
  9.0 2.5 %collective-permute-done.near1_ref = s32[4,2]{1,0:T(4,128)S(1)} collective-permute-done((s32[4,2]{1,0:T(4,128)S(1)}, s32[4,2]{1,0:T(4,128)S(1)}, u32[]{:S(2)}, u32[]{:S(2)}) %collective-permute-start) | collective-permute-done | bytes 64 | tf_op jit(solution)/shard_map/ppermute | solution.py:480
  11.4 0.0 copy-start.7
  11.4 0.0 copy-done.6
  11.4 0.6 copy-done.7
  12.0 52.5 %shard_map.136 = (bf16[8,128,128]{2,1,0:T(8,128)(2,1)}, bf16[8,128,128]{2,1,0:T(8,128)(2,1)}, f32[256,128]{1,0:T(8,128)}, f32[128,128]{1,0:T(8,128)}, f32[384,128]{1,0:T(8,128)}, /*index=5*/f32[128,128]{1,0:T(8,128)}) custom-call(s32[1]{0:T(128)S(6)} %copy.25.count_ref, s32[16,2]{1,0:T(8,128)} %copy.17.inner_ref, s32[8,2]{1,0:T(8,128)} %copy-done.5, ...), custom_call_target="tpu_custom_call" | custom-call | tf_op jit(solution)/shard_map/pallas_call | solution.py:495
  64.5 0.0 copy-start
  64.6 1.7 %copy.26 = bf16[1,1,8,128,128]{4,3,2,1,0:T(8,128)(2,1)} copy(bf16[1,1,8,128,128]{4,3,2,1,0:T(8,128)(2,1)} %bitcast.5) | data formatting | bytes 524288
  66.3 0.0 copy-done
  66.3 0.0 copy-start.2
  66.3 0.7 %copy.27 = bf16[1,1,8,128,128]{4,3,2,1,0:T(8,128)(2,1)} copy(bf16[1,1,8,128,128]{4,3,2,1,0:T(8,128)(2,1)S(1)} %bitcast.4) | data formatting | bytes 524288
  67.0 0.3 copy-done.2
  67.3 0.0 copy-start.4
  67.3 0.0 copy-start.1
  67.3 0.7 copy.28
  67.9 0.2 copy-done.4
  68.1 0.6 copy.29
  68.8 0.0 copy-done.1
  68.8 0.0 copy-start.3
  68.8 0.7 copy.30
  69.4 0.2 copy-done.3
  69.6 0.6 copy.31
  (1 shorter events, 0.0 us)
Async XLA Ops:
  1.4 0.6 copy-start.5
  2.0 7.0 %collective-permute-start.1 = (s32[4,2]{1,0:T(4,128)S(1)}, s32[4,2]{1,0:T(4,128)S(1)}, u32[]{:S(2)}, u32[]{:S(2)}) collective-permute-start(s32[4,2]{1,0:T(4,128)S(1)} %get-tuple-element.18), channel_id=1, source_target_pairs={{0,16},{8,24},{16,0},{24,8},{1,17},{9,25},{17,1},{25,9},{2,18},{10... | collective-permute-start | bytes 104 | tf_op jit(solution)/shard_map/ppermute | solution.py:480
  6.0 2.2 %copy-start.8 = (s32[16,2]{0,1:T(2,128)S(1)}, s32[16,2]{0,1:T(2,128)}, u32[]{:S(2)}) copy-start(s32[16,2]{0,1:T(2,128)} %param.16) | copy-start | bytes 388
  6.0 5.4 %collective-permute-start = (s32[4,2]{1,0:T(4,128)S(1)}, s32[4,2]{1,0:T(4,128)S(1)}, u32[]{:S(2)}, u32[]{:S(2)}) collective-permute-start(s32[4,2]{1,0:T(4,128)S(1)} %get-tuple-element.19), channel_id=1, source_target_pairs={{0,8},{8,16},{16,24},{24,0},{1,9},{9,17},{17,25},{25,1},{2,10},{10... | collective-permute-start | bytes 104 | tf_op jit(solution)/shard_map/ppermute | solution.py:480
  9.0 2.5 %copy-start.6 = (s32[4,2]{1,0:T(4,128)}, s32[4,2]{1,0:T(4,128)S(1)}, u32[]{:S(2)}) copy-start(s32[4,2]{1,0:T(4,128)S(1)} %collective-permute-done.1.near2_ref) | copy-start | bytes 100
  11.4 0.6 copy-start.7
  64.5 1.7 %copy-start = (bf16[8,128,128]{2,1,0:T(8,128)(2,1)S(1)}, bf16[8,128,128]{2,1,0:T(8,128)(2,1)}, u32[]{:S(2)}) copy-start(bf16[8,128,128]{2,1,0:T(8,128)(2,1)} %get-tuple-element.13) | copy-start | bytes 786436
  66.3 1.0 %copy-start.2 = (f32[256,128]{1,0:T(8,128)S(1)}, f32[256,128]{1,0:T(8,128)}, u32[]{:S(2)}) copy-start(f32[256,128]{1,0:T(8,128)} %get-tuple-element.28) | copy-start | bytes 393220
  67.3 0.9 %copy-start.4 = (f32[128,128]{1,0:T(8,128)S(1)}, f32[128,128]{1,0:T(8,128)}, u32[]{:S(2)}) copy-start(f32[128,128]{1,0:T(8,128)} %get-tuple-element.29) | copy-start | bytes 196612
  67.3 1.5 %copy-start.1 = (f32[384,128]{1,0:T(8,128)S(1)}, f32[384,128]{1,0:T(8,128)}, u32[]{:S(2)}) copy-start(f32[384,128]{1,0:T(8,128)} %get-tuple-element.30) | copy-start | bytes 589828
  68.8 0.9 %copy-start.3 = (f32[128,128]{1,0:T(8,128)S(1)}, f32[128,128]{1,0:T(8,128)}, u32[]{:S(2)}) copy-start(f32[128,128]{1,0:T(8,128)} %get-tuple-element.31) | copy-start | bytes 196612

commit v2 on v1

--- a/solution.py
+++ b/solution.py
@@ -10,7 +10,7 @@
 
 BND = 4
 REACH = 2
-CHUNKS = 2
+CHUNKS = 4
 FWD_TILE = 32
 BWD_TILE = 16
 MESH = pl.DeviceIdType.MESH
@@ -37,24 +37,19 @@
 def layer_kernel(
     sizes,
     offs,
-    scale,
     count_ref,
     inner_ref,
     outer_ref,
-    near1_ref,
-    near2_ref,
-    state_ref,
-    cot_ref,
-    ef_ref,
-    es_ref,
-    nf_ref,
-    ns_ref,
+    state_any,
+    cot_any,
+    ef_any,
+    es_any,
+    nf_any,
+    ns_any,
     upd_ref,
     sgrad_ref,
-    efg_ref,
-    esg_ref,
-    nfg_ref,
-    nsg_ref,
+    wfin,
+    near,
     wd_s,
     wa_s,
     wc_s,
@@ -68,6 +63,9 @@
     meanb,
     pre,
     cotg,
+    hiddenb,
+    gradb,
+    fgradb,
     mpart,
     mrecv,
     mgrad,
@@ -83,7 +81,6 @@
     wrecv_e,
     wdom_n,
     wdom_e,
-    wfin,
     halo_ss,
     halo_rs,
     rs1_ss,
@@ -102,12 +99,21 @@
     wd_rs,
     wg_ss,
     wg_rs,
+    near_ss,
+    near_rs,
+    state_ref,
+    cot_ref,
+    ef_ref,
+    es_ref,
+    nf_ref,
+    ns_ref,
+    load_s,
 ):
     n_dom, n_lev, n_mem = sizes
     n_grp = n_lev * n_mem
     blocks, rows, h = state_ref.shape
-    inner = inner_ref.shape[0]
-    per = outer_ref.shape[0] // REACH
+    inner = inner_ref.shape[1]
+    per = outer_ref.shape[1] // REACH
     chunk = rows // CHUNKS
     share = blocks // n_lev
     dom = lax.axis_index("dom")
@@ -135,6 +141,21 @@
         copy.start()
         return copy
 
+    loads = []
+    for i, (src, dst) in enumerate(
+        (
+            (state_any, state_ref),
+            (ef_any, ef_ref),
+            (cot_any, cot_ref),
+            (ns_any, ns_ref),
+            (nf_any, nf_ref),
+            (es_any, es_ref),
+        )
+    ):
+        load = pltpu.make_async_copy(src, dst, load_s.at[i])
+        load.start()
+        loads.append(load)
+
     barrier = pltpu.get_barrier_semaphore()
     for o in range(1, n_dom):
         pl.semaphore_signal(barrier, inc=1, device_id=dom_dev(o), device_id_type=MESH)
@@ -144,26 +165,18 @@
     live = count_ref[0]
     for f in range(inner):
         m = jnp.where(f < live, 1.0, 0.0).astype(F32)
-        a, c = inner_ref[f, 0], inner_ref[f, 1]
+        a, c = inner_ref[0, f], inner_ref[1, f]
         for b in range(blocks):
             wa = jnp.where(a == b, m, 0.0)
             wc = jnp.where(c == b, m, 0.0)
             wa_s[f * blocks + b] = wa
             wc_s[f * blocks + b] = wc
             wd_s[f * blocks + b] = wa - wc
-    outer = []
-    for o in range(1, REACH + 1):
-        near = near1_ref if o == 1 else near2_ref
-        ahead = blocks + BND * offs.index(o % n_dom)
-        behind = blocks + BND * offs.index(-o % n_dom)
-        for j in range(per):
-            outer.append((outer_ref[(o - 1) * per + j, 0], ahead + outer_ref[(o - 1) * per + j, 1]))
-            outer.append((near[j, 1], behind + near[j, 0]))
-    for f, (a, _) in enumerate(outer):
-        for b in range(BND):
-            wo_s[f * BND + b] = jnp.where(a == b, 1.0, 0.0).astype(F32)
-
     pl.semaphore_wait(barrier, n_dom - 1 + n_grp - 1)
+    near_c = [
+        remote(outer_ref, near.at[o - 1], near_ss.at[o - 1], near_rs.at[o - 1], dom_dev(o))
+        for o in range(1, REACH + 1)
+    ]
 
     halo_c = []
     for c in range(CHUNKS):
@@ -171,7 +184,7 @@
         halo_c.append(
             [
                 remote(
-                    state_ref.at[pl.ds(0, BND), rc],
+                    state_any.at[pl.ds(0, BND), rc],
                     halo.at[c, s],
                     halo_ss.at[c * len(offs) + s],
                     halo_rs.at[c * len(offs) + s],
@@ -181,6 +194,8 @@
             ]
         )
 
+    for load in loads:
+        load.wait()
     ef_wide = jnp.concatenate([ef_ref[:h], ef_ref[h:]], axis=1)
     es = es_ref[...]
     ns = ns_ref[...]
@@ -220,7 +235,7 @@
     def put_rows(ref, c, value):
         ref[:, c * chunk : (c + 1) * chunk] = value.reshape(-1, chunk, value.shape[-1])
 
-    inner_faces = [(inner_ref[f, 0], inner_ref[f, 1]) for f in range(inner)]
+    inner_faces = [(inner_ref[0, f], inner_ref[1, f]) for f in range(inner)]
     for c in range(CHUNKS):
         tab[:blocks, c * chunk : (c + 1) * chunk] = mm(rows_of(state_ref, c), ef_wide).reshape(
             blocks, chunk, 2 * h
@@ -267,6 +282,20 @@
             for k in range(1, n_lev)
         ]
 
+    for copy in near_c:
+        copy.wait_recv()
+    outer = []
+    for o in range(1, REACH + 1):
+        ahead = blocks + BND * offs.index(o % n_dom)
+        behind = blocks + BND * offs.index(-o % n_dom)
+        for j in range(per):
+            i = (o - 1) * per + j
+            outer.append((outer_ref[0, i], ahead + outer_ref[1, i]))
+            outer.append((near[o - 1, 1, i], behind + near[o - 1, 0, i]))
+    for f, (a, _) in enumerate(outer):
+        for b in range(BND):
+            wo_s[f * BND + b] = jnp.where(a == b, 1.0, 0.0).astype(F32)
+
     rs1 = []
     for c in range(CHUNKS):
         for copy in halo_c[c]:
@@ -289,38 +318,49 @@
     for c in range(CHUNKS):
         for copy in ag1[c]:
             copy.wait_recv()
-        mean = meanb[c].reshape(-1, h)
-        z = rows_of(pre, c) + mm(mean, n2)
+        z = rows_of(pre, c) + mm(meanb[c].reshape(-1, h), n2)
         g = gate(z)
         s = z * g
-        hidden = s.astype(BF16)
         grad = (rows_of(cotg, c) * (g + s - s * g)).astype(BF16)
         mpart[c] = mm_nt(grad, n2).astype(BF16).reshape(blocks, chunk, h)
         rs2.append(scatter(mpart, mrecv, rs2_ss, rs2_rs, c))
+        hiddenb[c] = s.astype(BF16).reshape(blocks, chunk, h)
+        gradb[c] = grad.reshape(blocks, chunk, h)
+
+    def add_weights(c, first, parts):
+        for i, part in enumerate(parts):
+            at = slice((first + i) * h, (first + i + 1) * h)
+            wacc[at] = part if c == 0 else wacc[at] + part
+
+    ag2 = []
+    for c in range(CHUNKS):
         state = rows_of(state_ref, c)
-        cot = rows_of(cot_ref, c)
-        put_rows(upd_ref, c, (state.astype(F32) + mm(hidden, ns)).astype(BF16))
-        put_rows(pre, c, cot.astype(F32) + mm_nt(grad, n0))
+        grad = gradb[c].reshape(-1, h)
         put_rows(fpart, c, mm_nt(grad, n1))
-        parts = (
-            mm_tn(state, grad),
-            mm_tn(fluxb[c].reshape(-1, h), grad),
-            mm_tn(mean, grad),
-            mm_tn(hidden, cot),
-        )
-        for i, part in enumerate(parts):
-            at = slice(i * h, (i + 1) * h)
-            wacc[at] = part if c == 0 else wacc[at] + part
-    ag2 = [
-        reduce_spread(rs2[c], mpart, mrecv, mgrad, ag2_ss, ag2_rs, c) for c in range(CHUNKS)
-    ]
+        put_rows(
+            upd_ref,
+            c,
+            (state.astype(F32) + mm(hiddenb[c].reshape(-1, h), ns)).astype(BF16),
+        )
+        ag2.append(reduce_spread(rs2[c], mpart, mrecv, mgrad, ag2_ss, ag2_rs, c))
     back = []
     for c in range(CHUNKS):
+        node_grad = gradb[c].reshape(-1, h)
+        add_weights(
+            c,
+            0,
+            (
+                mm_tn(rows_of(state_ref, c), node_grad),
+                mm_tn(fluxb[c].reshape(-1, h), node_grad),
+                mm_tn(meanb[c].reshape(-1, h), node_grad),
+                mm_tn(hiddenb[c].reshape(-1, h), rows_of(cot_ref, c)),
+            ),
+        )
         for copy in ag2[c]:
             copy.wait_recv()
         grad = (rows_of(fpart, c) + mgrad[c].reshape(-1, h).astype(F32)).astype(BF16)
+        fgradb[c] = grad.reshape(blocks, chunk, h)
         wide = mm_nt(grad, es).reshape(blocks, chunk, h)
-        gw[:blocks, c * chunk : (c + 1) * chunk] = wide
         gwsend[c] = wide[:BND].astype(BF16)
         back.append(
             [
@@ -334,9 +374,9 @@
                 for s, o in enumerate(offs)
             ]
         )
-        part = mm_tn(rows_of(nd, c).astype(BF16), grad)
-        at = slice(4 * h, 5 * h)
-        wacc[at] = part if c == 0 else wacc[at] + part
+        gw[:blocks, c * chunk : (c + 1) * chunk] = wide
+    for c in range(CHUNKS):
+        add_weights(c, 4, (mm_tn(rows_of(nd, c).astype(BF16), fgradb[c].reshape(-1, h)),))
 
     def weights_out(first, count, got, sem):
         size = count // n_grp
@@ -431,27 +471,61 @@
         a = rows_of(acc_a, c).astype(BF16)
         b = rows_of(acc_b, c).astype(BF16)
         state = rows_of(state_ref, c)
-        for i, part in enumerate((mm_tn(state, a), mm_tn(state, b))):
-            at = slice((5 + i) * h, (6 + i) * h)
-            wacc[at] = part if c == 0 else wacc[at] + part
-        if c == CHUNKS - 1:
-            e1 = weights_out(n_rows, 2 * h, wrecv_e, 1)
-            w3 = weights_in(w2, 0, n_rows, wdom_n, 0)
-        total = rows_of(pre, c) + mm_nt(a, ef_ref[:h]) + mm_nt(b, ef_ref[h:])
+        add_weights(c, 5, (mm_tn(state, a), mm_tn(state, b)))
+    e1 = weights_out(n_rows, 2 * h, wrecv_e, 1)
+    w3 = weights_in(w2, 0, n_rows, wdom_n, 0)
+
+    def finish(c):
+        a = rows_of(acc_a, c).astype(BF16)
+        b = rows_of(acc_b, c).astype(BF16)
+        total = rows_of(cot_ref, c).astype(F32) + mm_nt(gradb[c].reshape(-1, h), n0)
+        total = total + mm_nt(a, ef_ref[:h]) + mm_nt(b, ef_ref[h:])
         put_rows(sgrad_ref, c, total.astype(BF16))
+
+    half = CHUNKS // 2
+    for c in range(half):
+        finish(c)
     e2 = weights_mid(e1, n_rows, 2 * h, wrecv_e, wdom_e, 1)
+    for c in range(half, CHUNKS):
+        finish(c)
     for copy in w3:
         copy.wait_recv()
-    nfg_ref[...] = wfin[: 3 * h].astype(F32) * scale
-    nsg_ref[...] = wfin[3 * h : 4 * h].astype(F32) * scale
-    esg_ref[...] = wfin[4 * h : 5 * h].astype(F32) * scale
     e3 = weights_in(e2, n_rows, 2 * h, wdom_e, 1)
-    for group in halo_c + rs1 + ag1 + rs2 + ag2 + back + [w1, w2, w3, e1, e2]:
+    for group in [near_c] + halo_c + rs1 + ag1 + rs2 + ag2 + back + [w1, w2, w3, e1, e2]:
         for copy in group:
             copy.wait_send()
     for copy in e3:
         copy.wait()
-    efg_ref[...] = wfin[5 * h :].astype(F32) * scale
+
+
+def output_kernel(
+    scale,
+    upd_in,
+    sgrad_in,
+    w_any,
+    upd_ref,
+    sgrad_ref,
+    efg_ref,
+    esg_ref,
+    nfg_ref,
+    nsg_ref,
+    w_in,
+    load_s,
+):
+    h = upd_in.shape[2]
+    pairs = ((w_any, w_in), (upd_in, upd_ref), (sgrad_in, sgrad_ref))
+    loads = [
+        pltpu.make_async_copy(src, dst, load_s.at[i]) for i, (src, dst) in enumerate(pairs)
+    ]
+    for load in loads:
+        load.start()
+    loads[0].wait()
+    nfg_ref[...] = w_in[: 3 * h].astype(F32) * scale
+    nsg_ref[...] = w_in[3 * h : 4 * h].astype(F32) * scale
+    esg_ref[...] = w_in[4 * h : 5 * h].astype(F32) * scale
+    efg_ref[...] = w_in[5 * h :].astype(F32) * scale
+    for load in loads[1:]:
+        load.wait()
 
 
 def shards(
@@ -474,10 +548,6 @@
     outer = outer_pairs.shape[0]
     per = outer // REACH
     offs = sorted({s * o % n_dom for o in range(1, REACH + 1) for s in (1, -1)})
-    near = []
-    for o in range(1, REACH + 1):
-        hops = [(i, (i + o) % n_dom) for i in range(n_dom)]
-        near.append(lax.ppermute(outer_pairs[(o - 1) * per : o * per], "dom", hops))
     scale = 1.0 / math.sqrt(n_mem * n_lev * blocks * n_dom * rows)
     faces = inner + 2 * outer
     chunk = rows // CHUNKS
@@ -492,19 +562,17 @@
     cut = (CHUNKS, blocks, chunk, h)
     smem = pl.BlockSpec(memory_space=pltpu.SMEM)
     vmem = pl.BlockSpec(memory_space=pltpu.VMEM)
-    upd, sgrad, efg, esg, nfg, nsg = pl.pallas_call(
-        functools.partial(layer_kernel, (n_dom, n_lev, n_mem), offs, scale),
+    held = pl.pallas_call(
+        functools.partial(layer_kernel, (n_dom, n_lev, n_mem), offs),
         out_shape=(
             jax.ShapeDtypeStruct(full, BF16),
             jax.ShapeDtypeStruct(full, BF16),
-            jax.ShapeDtypeStruct((2 * h, h), F32),
-            jax.ShapeDtypeStruct((h, h), F32),
-            jax.ShapeDtypeStruct((3 * h, h), F32),
-            jax.ShapeDtypeStruct((h, h), F32),
+            jax.ShapeDtypeStruct((7 * h, h), BF16),
         ),
-        in_specs=[smem] * 5 + [vmem] * 6,
-        out_specs=(vmem,) * 6,
+        in_specs=[smem] * 3 + [pl.BlockSpec(memory_space=pl.ANY)] * 6,
+        out_specs=(vmem,) * 3,
         scratch_shapes=[
+            pltpu.SMEM((REACH, 2, outer), jnp.int32),
             pltpu.SMEM((inner * blocks,), F32),
             pltpu.SMEM((inner * blocks,), F32),
             pltpu.SMEM((inner * blocks,), F32),
@@ -518,6 +586,9 @@
             pltpu.VMEM(cut, BF16),
             pltpu.VMEM(full, F32),
             pltpu.VMEM(full, F32),
+            pltpu.VMEM(cut, BF16),
+            pltpu.VMEM(cut, BF16),
+            pltpu.VMEM(cut, BF16),
             pltpu.VMEM(cut, BF16),
             pltpu.VMEM((CHUNKS, n_lev - 1, share, chunk, h), BF16),
             pltpu.VMEM(cut, BF16),
@@ -533,7 +604,6 @@
             pltpu.VMEM((n_grp - 1, size_e, h), BF16),
             pltpu.VMEM((n_dom, size_n, h), BF16),
             pltpu.VMEM((n_dom, size_e, h), BF16),
-            pltpu.VMEM((7 * h, h), BF16),
             dma((CHUNKS * slots,)),
             dma((CHUNKS * slots,)),
             *lev_sems,
@@ -545,15 +615,23 @@
             dma((2, n_dom - 1)),
             dma((2, n_grp - 1)),
             dma((2, n_grp - 1)),
+            dma((REACH,)),
+            dma((REACH,)),
+            pltpu.VMEM(full, BF16),
+            pltpu.VMEM(full, BF16),
+            pltpu.VMEM((2 * h, h), BF16),
+            pltpu.VMEM((h, h), BF16),
+            pltpu.VMEM((3 * h, h), BF16),
+            pltpu.VMEM((h, h), BF16),
+            dma((6,)),
         ],
         compiler_params=pltpu.CompilerParams(
             collective_id=0, has_side_effects=True, vmem_limit_bytes=56 * 1024 * 1024
         ),
     )(
         inner_count,
-        inner_pairs,
-        outer_pairs,
-        *near,
+        inner_pairs.T,
+        outer_pairs.T,
         state,
         cot,
         edge_first,
@@ -561,6 +639,21 @@
         node_first,
         node_second,
     )
+    upd, sgrad, efg, esg, nfg, nsg = pl.pallas_call(
+        functools.partial(output_kernel, scale),
+        out_shape=(
+            jax.ShapeDtypeStruct(full, BF16),
+            jax.ShapeDtypeStruct(full, BF16),
+            jax.ShapeDtypeStruct((2 * h, h), F32),
+            jax.ShapeDtypeStruct((h, h), F32),
+            jax.ShapeDtypeStruct((3 * h, h), F32),
+            jax.ShapeDtypeStruct((h, h), F32),
+        ),
+        in_specs=[pl.BlockSpec(memory_space=pl.ANY)] * 3,
+        out_specs=(vmem,) * 6,
+        scratch_shapes=[pltpu.VMEM((7 * h, h), BF16), dma((3,))],
+        compiler_params=pltpu.CompilerParams(vmem_limit_bytes=60 * 1024 * 1024),
+    )(*held)
     return (upd[None, None], sgrad[None, None], efg, esg, nfg, nsg)
 
 

time: 70.5 us -> 58.2 us (0.83)
  local copies, waits for them, and re-layouts: 8.31 us -> 0 us
  starting transfers between devices: 5.64 us -> 0 us
  Pallas kernels: 52.5 us -> 56.7 us
  waiting for transfers between devices: 2.46 us -> 0 us
    unnamed x26 -> x0, local copies, waits for them, and re-layouts: 8.3 us -> none
    ppermute x2 -> x0, starting transfers between devices: 5.64 us -> none  [shards(): near.append(lax.ppermute(outer_pairs[(o - 1) * per:o * per], 'dom', hops))]
    ppermute x2 -> x0, waiting for transfers between devices: 2.46 us -> none  [shards(): near.append(lax.ppermute(outer_pairs[(o - 1) * per:o * per], 'dom', hops))]
    pallas_call x0 -> x1, Pallas kernels: none -> 2.11 us  [shards(): pl.pallas_call(functools.partial(output_kernel, scale), out_shape=(jax.Sh...]
    pallas_call x1, Pallas kernels: 52.5 us -> 54.6 us  [shards(): pl.pallas_call(functools.partial(layer_kernel, (n_dom, n_lev, n_mem), off...]
  transfers between devices with their start and end apart: 2 -> 0, of which waited for: 1 -> 0; matrix products, arithmetic and copies ran while one was open for 1% -> 0% of each run, Pallas kernels for 0% -> 0%
where the time goes in v2:
time: 58.2 us; the launch traced here: 58 us
  Pallas kernels  56.7 us (97%)
  between operations  1.29 us (2%)
    pallas_call x1, Pallas kernels, shards(): pl.pallas_call(functools.partial(layer_kernel, (n_dom, n_lev, n_mem), off...  54.6 us
    pallas_call x1, Pallas kernels, shards(): pl.pallas_call(functools.partial(output_kernel, scale), out_shape=(jax.Sh...  2.11 us

profile of v2, /device:TPU:0, one launch (start us, length us, event | category | flops | bytes accessed | tf_op | source)
XLA Modules:
  0.0 58.0 jit_solution(12458048231819133095)
XLA Ops:
  1.3 54.6 %shard_map.136 = (bf16[8,128,128]{2,1,0:T(8,128)(2,1)}, bf16[8,128,128]{2,1,0:T(8,128)(2,1)}, bf16[896,128]{1,0:T(8,128)(2,1)}) custom-call(s32[1]{0:T(128)S(6)} %copy.15.count_ref, s32[2,16]{1,0:T(2,128)} %bitcast.8, s32[2,8]{1,0:T(2,128)} %bitcast.9, bf16[8,128,128]{2,1,0:T(8,128)(2,1)} %bitcast.6, bf16[8,128,128]{2,1,0:T(8,128)(2,1)} %bitcast.7, ...), custom_call_target="tpu_custom_call" | custom-call | tf_op jit(solution)/shard_map/pallas_call | solution.py:565
  55.9 2.1 %shard_map.137 = (bf16[8,128,128]{2,1,0:T(8,128)(2,1)}, bf16[8,128,128]{2,1,0:T(8,128)(2,1)}, f32[256,128]{1,0:T(8,128)}, f32[128,128]{1,0:T(8,128)}, f32[384,128]{1,0:T(8,128)}, /*index=5*/f32[128,128]{1,0:T(8,128)}) custom-call(bf16[8,128,128]{2,1,0:T(8,128)(2,1)} %get-tuple-element.15.upd_in, bf16[8,128,128]{2,1,0:T(8,128)(2,1)} %get-tuple-element.16.sgrad_in, ...), custom_call_target="tpu_custom_call" | custom-call | tf_op jit(solution)/shard_map/pallas_call | solution.py:642
